TPU v7x, 512 devices: a whole 4x4x16 slice. The times are simulated.
512 devices in a mesh: dom: 128 (over z, y, core), src: 4 (over x).
Axes of the slice: x: 4, y: 4, z: 16, core: 2. Of those that a mesh axis runs over, the one named last changes fastest.
Arguments:
- features: bfloat16 [524288, 256], P(('dom', 'src')), may hold values from -6 to 6
- cotangent: bfloat16 [524288, 256], P(('dom', 'src')), may hold values from -6 to 6
- w_self: bfloat16 [256, 256], replicated, may hold values from -0.375 to 0.375
- w_neigh: bfloat16 [256, 256], replicated, may hold values from -0.375 to 0.375
- bias: bfloat16 [256], replicated, may hold values from -3 to 3
- send_rows: int32 [128, 4, 128, 8], P('dom', 'src'), may hold values from -1 to 1023, as said below
- edge_src: int32 [128, 4, 8192], P('dom', 'src'), may hold values from 0 to 2047, as said below
- edge_dst: int32 [128, 4, 8192], P('dom', 'src'), may hold values from 0 to 4095
- tile_count: int32 [128, 4], P('dom', 'src'), may hold values from 16 to 64, as said below
Outputs:
- activations: bfloat16 [524288, 256], P(('dom', 'src'))
- feature_grad: float32 [524288, 256], P(('dom', 'src'))
Inputs may be any that keep to these rules, and one draw needn't show every extreme that they name: `send_rows`: slots of a list are filled from the first one; some list of every owner is full; an account's own part sends it nothing. `edge_src`: every edge refers to a local row or to a filled slot. Edge slots after the first tile_count * 128 are ignored.
All inputs are finite; a program needn't handle non-finite values.
Results may differ from a plain program's by a relative error of at most 0.009.
Values may be sent and summed in bfloat16 or wider, within the bound.
No kernel may reach another device: no remote copies, remote signals or barrier semaphores. Data moves between devices by JAX's collectives and lax.ppermute only.
A program may use at most 64 MiB of HBM per device.

v0:
```python
import jax
import jax.numpy as jnp
from jax import lax
from jax.sharding import PartitionSpec as P


def local(features, cotangent, w_self, w_neigh, bias, send_rows, edge_src, edge_dst, tile_count):
    node_rows = features.shape[0]
    feature_width = features.shape[1]
    peer_total = lax.axis_size("dom")
    senders = send_rows[0, 0]
    capacity = senders.shape[1]
    halo_total = peer_total * capacity
    sources = edge_src[0, 0]
    targets = edge_dst[0, 0]
    edge_total = sources.shape[0]
    part_total = node_rows * lax.axis_size("src")
    active = jnp.arange(edge_total) // 128 < tile_count[0, 0]
    filled = senders >= 0
    zero_half = jnp.zeros((), jnp.bfloat16)
    picked = jnp.where(filled[:, :, None], features[jnp.maximum(senders, 0)], zero_half)
    counts = jnp.zeros((part_total,), jnp.float32).at[targets].add(active.astype(jnp.float32))
    degree_all = lax.psum(counts, "src")
    inverse_all = 1.0 / jnp.maximum(degree_all, 1.0)
    inverse = lax.dynamic_slice_in_dim(inverse_all, lax.axis_index("src") * node_rows, node_rows)
    remote = lax.all_to_all(picked, "dom", split_axis=0, concat_axis=0, tiled=True).reshape(
        halo_total, feature_width
    )
    table = jnp.concatenate([features, remote], axis=0)
    taken = jnp.where(active[:, None], table[sources], zero_half)
    partial_value = (
        jnp.zeros((part_total, feature_width), jnp.float32)
        .at[targets]
        .add(taken.astype(jnp.float32))
    )
    totals = lax.psum_scatter(
        partial_value.astype(jnp.bfloat16), "src", scatter_dimension=0, tiled=True
    ).astype(jnp.float32)
    neighbour_mean = (totals * inverse[:, None]).astype(jnp.bfloat16)
    preact = (
        jnp.dot(features, w_self, preferred_element_type=jnp.float32)
        + jnp.dot(neighbour_mean, w_neigh, preferred_element_type=jnp.float32)
        + bias.astype(jnp.float32)
    )
    sigma = jax.nn.sigmoid(preact)
    outputs = (preact * sigma).astype(jnp.bfloat16)
    slope = sigma * (1.0 + preact * (1.0 - sigma))
    upstream = (cotangent.astype(jnp.float32) * slope).astype(jnp.bfloat16)
    grad_own = jnp.dot(upstream, w_self.T, preferred_element_type=jnp.float32)
    scaled = (
        jnp.dot(upstream, w_neigh.T, preferred_element_type=jnp.float32) * inverse[:, None]
    ).astype(jnp.bfloat16)
    spread = lax.all_gather(scaled, "src", axis=0, tiled=True)
    contrib = jnp.where(active[:, None], spread[targets], zero_half).astype(jnp.float32)
    grad_table = (
        jnp.zeros((node_rows + halo_total, feature_width), jnp.float32).at[sources].add(contrib)
    )
    remote_grad = grad_table[node_rows:]
    local_grad = grad_table[:node_rows]
    returned = lax.all_to_all(
        remote_grad.reshape(peer_total, capacity, feature_width).astype(jnp.bfloat16),
        "dom",
        split_axis=0,
        concat_axis=0,
        tiled=True,
    ).astype(jnp.float32)
    back_rows = jnp.where(filled, senders, node_rows)
    incoming = (
        jnp.zeros((node_rows, feature_width), jnp.float32).at[back_rows].add(returned, mode="drop")
    )
    return (outputs, grad_own + local_grad + incoming)


def solution(mesh):
    placed = (
        P(("dom", "src"), None),
        P(("dom", "src"), None),
        P(),
        P(),
        P(),
        P("dom", "src", None, None),
        P("dom", "src", None),
        P("dom", "src", None),
        P("dom", "src"),
    )
    return jax.shard_map(
        local,
        mesh=mesh,
        in_specs=placed,
        out_specs=(P(("dom", "src"), None), P(("dom", "src"), None)),
        check_vma=False,
    )
```

profile of v0, /device:TPU:33, one launch (start us, length us, event | category | flops | bytes accessed | tf_op | source)
XLA Modules:
  0.0 406.9 jit_solution(14900899894254317384)
XLA Ops:
  7.2 0.0 copy-start
  7.2 0.0 copy-start.1
  7.2 0.0 copy-start.3
  7.2 0.0 copy-start.4
  7.2 0.8 compare_select_fusion.2
  8.0 0.7 compare_bitcast_fusion
  8.7 0.1 copy.13
  8.8 0.1 reshape.127
  8.9 0.1 copy.12
  9.0 4.6 %gather_fusion = bf16[1024,256]{1,0:T(8,128)(2,1)S(1)} fusion(bf16[1024,256]{1,0:T(8,128)(2,1)} %param.9, s32[1024]{0:T(1024)S(1)} %broadcast_clamp_fusion.2), kind=kCustom, calls=%fused_computation | custom fusion | bytes 1052672 | tf_op jit(solution)/shard_map/gather | solution.py:21
  13.6 1.0 bitcast_select_fusion
  14.6 19.5 %all-to-all-start = ((bf16[128,8,256]{2,1,0:T(8,128)(2,1)}), bf16[128,8,256]{2,1,0:T(8,128)(2,1)S(1)}, u32[]{:S(2)}, u32[]{:S(2)}) async-start(bf16[128,8,256]{2,1,0:T(8,128)(2,1)} %bitcast_select_fusion), calls=%async_computation | async-start | bytes 1048576 | tf_op jit(solution)/shard_map/all_to_all | solution.py:26
  34.1 0.0 reduce-scatter.2.cloned.1.call-start
  34.8 0.0 copy-done.3
  34.8 0.0 copy-done.4
  34.9 32.7 %all-to-all-done = bf16[128,8,256]{2,1,0:T(8,128)(2,1)S(1)} async-done(((bf16[128,8,256]{2,1,0:T(8,128)(2,1)}), bf16[128,8,256]{2,1,0:T(8,128)(2,1)S(1)}, u32[]{:S(2)}, u32[]{:S(2)}) %all-to-all-start) | async-done | bytes 524320 | tf_op jit(solution)/shard_map/all_to_all | solution.py:26
  67.6 0.0 copy-done.1
  67.6 0.1 pad_maximum_fusion
  67.7 76.8 %scatter_custom_fusion = f32[4096,256]{1,0:T(8,128)} fusion(s32[8192]{0:T(1024)S(1)} %bitcast.39, pred[8192]{0:T(1024)(128)(4,1)S(1)} %fusion.19, bf16[]{:T(256)} %constant.41.clone.1, f32[]{:T(128)} %constant.14.clone.1, bf16[2048,256]{1,0:T(8,128)(2,1)S(1)} %pad_maximum_fusion, s32[8192]{0:T(1024)S(1)} %broadcast_clamp_fusion.1), kind=kCustom, calls=%fused_computation.9 | custom fusion | flops 6291456 | bytes 5283846 | tf_op jit(solution)/shard_map/scatter-add | solution.py:34
  144.6 0.0 copy-start.6
  144.6 0.0 copy-start.2
  144.6 0.0 copy-start.5
  144.6 3.8 convert_element_type.41
  148.3 0.0 reduce-scatter.2.cloned.1.call-update
  148.4 0.0 all-gather.2.cloned.1.call-start
  148.4 43.2 %scatter_custom_fusion.1 = f32[4096]{0:T(1024)S(1)} fusion(s32[8192]{0:T(1024)S(1)} %bitcast.40, f32[8192]{0:T(1024)S(1)} %fusion.25, f32[]{:T(128)} %constant.14.clone.1), kind=kCustom, calls=%fused_computation.50 | custom fusion | flops 8192 | bytes 16388 | tf_op jit(solution)/shard_map/scatter-add | solution.py:22
  191.7 0.0 copy-done.6
  191.7 13.2 %psum.7 = f32[4096]{0:T(1024)S(1)} all-reduce(f32[4096]{0:T(1024)S(1)} %scatter_custom_fusion.1), channel_id=1, replica_groups=mesh['dom'=128,'src'=4] {'src'}, use_global_device_ids=true, to_apply=%region_3.4 | all-reduce | flops 4096 | bytes 32768 | tf_op jit(solution)/shard_map/psum | solution.py:23
  204.8 0.0 copy-done.2
  204.8 0.3 fusion.29
  205.1 0.0 reduce-scatter.2.cloned.1.call-done
  205.2 0.0 copy-done
  205.2 0.0 copy-done.5
  205.2 2.6 multiply_convert_fusion
  207.8 1.1 fusion.12
  208.9 0.0 all-gather.2.cloned.1.call-update
  208.9 31.2 %all-gather.2.cloned.1.call-done = bf16[4096,256]{1,0:T(8,128)(2,1)} async-done(((bf16[1024,256]{1,0:T(8,128)(2,1)}), bf16[4096,256]{1,0:T(8,128)(2,1)}) %all-gather.2.cloned.1.call-update) | async-done | bytes 2097168 | tf_op jit(solution)/shard_map/all_gather | solution.py:53
  240.1 100.4 %scatter_custom_fusion.2 = f32[2048,256]{1,0:T(8,128)S(1)} fusion(s32[8192]{0:T(1024)S(1)} %bitcast.38, pred[8192]{0:T(1024)(128)(4,1)S(1)} %fusion.19, bf16[]{:T(256)} %constant.41.clone.1, f32[]{:T(128)} %constant.14.clone.1, bf16[4096,256]{1,0:T(8,128)(2,1)} %all-gather.2.cloned.1.call-done, s32[8192]{0:T(1024)S(1)} %broadcast_clamp_fusion), kind=kCustom, calls=%fused_computation.7 | custom fusion | flops 6291456 | bytes 4235270 | tf_op jit(solution)/shard_map/scatter-add | solution.py:56
  340.5 0.8 fusion.16
  341.4 16.8 %all-to-all-start.1 = ((bf16[128,8,256]{2,1,0:T(8,128)(2,1)}), bf16[128,8,256]{2,1,0:T(8,128)(2,1)S(1)}, u32[]{:S(2)}, u32[]{:S(2)}) async-start(bf16[128,8,256]{2,1,0:T(8,128)(2,1)} %fusion.16), calls=%async_computation.2 | async-start | bytes 1048576 | tf_op jit(solution)/shard_map/all_to_all | solution.py:60
  358.2 0.1 copy.14
  358.3 0.1 reshape.175
  358.4 1.3 convolution_add_fusion
  359.7 32.1 %all-to-all-done.1 = bf16[128,8,256]{2,1,0:T(8,128)(2,1)S(1)} async-done(((bf16[128,8,256]{2,1,0:T(8,128)(2,1)}), bf16[128,8,256]{2,1,0:T(8,128)(2,1)S(1)}, u32[]{:S(2)}, u32[]{:S(2)}) %all-to-all-start.1) | async-done | bytes 524320 | tf_op jit(solution)/shard_map/all_to_all | solution.py:60
  391.8 8.3 %scatter_custom_fusion.3 = f32[1024,256]{1,0:T(8,128)} fusion(f32[1024,256]{1,0:T(8,128)} %convolution_add_fusion, s32[1024]{0:T(1024)S(1)} %reshape.175, bf16[128,8,256]{2,1,0:T(8,128)(2,1)S(1)} %all-to-all-done.1), kind=kCustom, calls=%fused_computation.25 | custom fusion | flops 524288 | bytes 1572864 | tf_op jit(solution)/shard_map/scatter-add | solution.py:69
  (9 shorter events, 0.1 us)
Async XLA Ops:
  7.2 198.0 %copy-start = (bf16[256,256]{1,0:T(8,128)(2,1)S(1)}, bf16[256,256]{1,0:T(8,128)(2,1)}, u32[]{:S(2)}) copy-start(bf16[256,256]{1,0:T(8,128)(2,1)} %param.12) | copy-start | bytes 393220
  7.2 60.5 %copy-start.1 = (bf16[1024,256]{1,0:T(8,128)(2,1)S(1)}, bf16[1024,256]{1,0:T(8,128)(2,1)}, u32[]{:S(2)}) copy-start(bf16[1024,256]{1,0:T(8,128)(2,1)} %param.9) | copy-start | bytes 1572868
  7.2 27.6 %copy-start.3 = (s32[1,1,8192]{2,1,0:T(1,128)S(1)}, s32[1,1,8192]{2,1,0:T(1,128)}, u32[]{:S(2)}) copy-start(s32[1,1,8192]{2,1,0:T(1,128)} %param.15) | copy-start | bytes 98308
  7.2 27.6 %copy-start.4 = (s32[1,1,8192]{2,1,0:T(1,128)S(1)}, s32[1,1,8192]{2,1,0:T(1,128)}, u32[]{:S(2)}) copy-start(s32[1,1,8192]{2,1,0:T(1,128)} %param.16) | copy-start | bytes 98308
  14.6 53.1 %all-to-all-start = ((bf16[128,8,256]{2,1,0:T(8,128)(2,1)}), bf16[128,8,256]{2,1,0:T(8,128)(2,1)S(1)}, u32[]{:S(2)}, u32[]{:S(2)}) async-start(bf16[128,8,256]{2,1,0:T(8,128)(2,1)} %bitcast_select_fusion), calls=%async_computation | async-start | bytes 1048576 | tf_op jit(solution)/shard_map/all_to_all | solution.py:26
  34.1 171.1 %reduce-scatter.2.cloned.1.call-start = ((), (), s32[]{:S(2)}) async-start(), calls=%async_computation.3 | async-start | bytes 2621440 | tf_op jit(solution)/shard_map/reduce_scatter | solution.py:36
  144.6 47.1 %copy-start.6 = (bf16[256]{0:T(256)(128)(2,1)S(1)}, bf16[256]{0:T(256)(128)(2,1)}, u32[]{:S(2)}) copy-start(bf16[256]{0:T(256)(128)(2,1)} %param.13) | copy-start | bytes 1540
  144.6 60.3 %copy-start.2 = (bf16[256,256]{1,0:T(8,128)(2,1)S(1)}, bf16[256,256]{1,0:T(8,128)(2,1)}, u32[]{:S(2)}) copy-start(bf16[256,256]{1,0:T(8,128)(2,1)} %param.11) | copy-start | bytes 393220
  144.6 60.6 %copy-start.5 = (bf16[1024,256]{1,0:T(8,128)(2,1)S(1)}, bf16[1024,256]{1,0:T(8,128)(2,1)}, u32[]{:S(2)}) copy-start(bf16[1024,256]{1,0:T(8,128)(2,1)} %param.10) | copy-start | bytes 1572868
  148.4 91.8 %all-gather.2.cloned.1.call-start = ((), (), s32[]{:S(2)}) async-start(), calls=%async_computation.4 | async-start | bytes 2621440 | tf_op jit(solution)/shard_map/all_gather | solution.py:53
  341.4 50.4 %all-to-all-start.1 = ((bf16[128,8,256]{2,1,0:T(8,128)(2,1)}), bf16[128,8,256]{2,1,0:T(8,128)(2,1)S(1)}, u32[]{:S(2)}, u32[]{:S(2)}) async-start(bf16[128,8,256]{2,1,0:T(8,128)(2,1)} %fusion.16), calls=%async_computation.2 | async-start | bytes 1048576 | tf_op jit(solution)/shard_map/all_to_all | solution.py:60
Sparse Core Ops, SparseCore 0:
  148.5 28.3 reduce-scatter.1
  209.0 31.0 all-gather.1
where the time goes:
time: 408 us; the launch traced here: 407 us
  other arithmetic  235 us (58%)
  waiting for transfers between devices  96.1 us (24%)
  starting transfers between devices  36.4 us (9%)
  between operations  14.9 us (4%)
  blocking collectives  13.2 us (3%)
  local copies, waits for them, and re-layouts  5.95 us (1%)
  matrix products  5.3 us (1%)
    scatter-add x1, other arithmetic, local(): jnp.zeros((node_rows + halo_total, feature_width), jnp.float32).at[sources]  100 us
    scatter-add x1, other arithmetic, local(): partial_value = jnp.zeros((part_total, feature_width), jnp.float32).at[ta...  76.8 us
    scatter-add x1, other arithmetic, local(): jnp.zeros((part_total,), jnp.float32).at[targets]  43.2 us
    all_to_all x1, waiting for transfers between devices, local(): lax.all_to_all(picked, 'dom', split_axis=0, concat_axis=0, tiled=True)  32.7 us
    all_to_all x1, waiting for transfers between devices, local(): lax.all_to_all(remote_grad.reshape(peer_total, capacity, feature_width).a...  32.1 us
    all_gather x1, waiting for transfers between devices, local(): spread = lax.all_gather(scaled, 'src', axis=0, tiled=True)  31.2 us
    all_to_all x1, starting transfers between devices, local(): lax.all_to_all(picked, 'dom', split_axis=0, concat_axis=0, tiled=True)  19.5 us
    all_to_all x1, starting transfers between devices, local(): lax.all_to_all(remote_grad.reshape(peer_total, capacity, feature_width).a...  16.8 us
  transfers between devices with their start and end apart: 4, of which 3 were waited for; matrix products, arithmetic and copies ran while one was open for 11% of the time, Pallas kernels for 0%

commit v1 on v0

--- a/solution.py
+++ b/solution.py
@@ -50,7 +50,9 @@
     scaled = (
         jnp.dot(upstream, w_neigh.T, preferred_element_type=jnp.float32) * inverse[:, None]
     ).astype(jnp.bfloat16)
-    spread = lax.all_gather(scaled, "src", axis=0, tiled=True)
+    spread = jnp.concatenate(
+        lax.all_to_all(jnp.stack([scaled] * lax.axis_size("src")), "src", 0, 0), axis=0
+    )
     contrib = jnp.where(active[:, None], spread[targets], zero_half).astype(jnp.float32)
     grad_table = (
         jnp.zeros((node_rows + halo_total, feature_width), jnp.float32).at[sources].add(contrib)

time: 408 us -> 373 us (0.914)
  other arithmetic: 235 us -> 209 us
  waiting for transfers between devices: 96.1 us -> 87.2 us
    all_gather x1 -> x0, waiting for transfers between devices: 31.2 us -> none  [local(): spread = lax.all_gather(scaled, 'src', axis=0, tiled=True)]
    scatter-add x1, other arithmetic: 100 us -> 76.1 us  [local(): jnp.zeros((node_rows + halo_total, feature_width), jnp.float32).at[sources]]
    all_to_all x0 -> x1, waiting for transfers between devices: none -> 22.6 us  [local(): lax.all_to_all(jnp.stack([scaled] * lax.axis_size('src')), 'src', 0, 0)]
    all_to_all x1, starting transfers between devices: 16.8 us -> 10.1 us  [local(): lax.all_to_all(remote_grad.reshape(peer_total, capacity, feature_width).a...]
  transfers between devices with their start and end apart: 4 -> 4, of which waited for: 3 -> 3; matrix products, arithmetic and copies ran while one was open for 11% -> 12% of each run, Pallas kernels for 0% -> 0%
where the time goes in v1:
time: 373 us; the launch traced here: 372 us
  other arithmetic  209 us (56%)
  waiting for transfers between devices  87.2 us (23%)
  starting transfers between devices  33.4 us (9%)
  between operations  14.9 us (4%)
  blocking collectives  13.1 us (4%)
  local copies, waits for them, and re-layouts  9.63 us (3%)
  matrix products  4.75 us (1%)
    scatter-add x1, other arithmetic, local(): partial_value = jnp.zeros((part_total, feature_width), jnp.float32).at[ta...  76.8 us
    scatter-add x1, other arithmetic, local(): jnp.zeros((node_rows + halo_total, feature_width), jnp.float32).at[sources]  76.1 us
    scatter-add x1, other arithmetic, local(): jnp.zeros((part_total,), jnp.float32).at[targets]  43.2 us
    all_to_all x1, waiting for transfers between devices, local(): lax.all_to_all(picked, 'dom', split_axis=0, concat_axis=0, tiled=True)  32.7 us
    all_to_all x1, waiting for transfers between devices, local(): lax.all_to_all(remote_grad.reshape(peer_total, capacity, feature_width).a...  31.8 us
    all_to_all x1, waiting for transfers between devices, local(): lax.all_to_all(jnp.stack([scaled] * lax.axis_size('src')), 'src', 0, 0)  22.6 us
    all_to_all x1, starting transfers between devices, local(): lax.all_to_all(picked, 'dom', split_axis=0, concat_axis=0, tiled=True)  19.5 us
    psum x1, blocking collectives, local(): degree_all = lax.psum(counts, 'src')  13.1 us
  transfers between devices with their start and end apart: 4, of which 3 were waited for; matrix products, arithmetic and copies ran while one was open for 12% of the time, Pallas kernels for 0%

profile of v1, /device:TPU:33, one launch (start us, length us, event | category | flops | bytes accessed | tf_op | source)
XLA Modules:
  0.0 372.0 jit_solution(9073737643823150255)
XLA Ops:
  7.2 0.0 copy-start
  7.2 0.0 copy-start.1
  7.2 0.0 copy-start.4
  7.2 0.0 copy-start.5
  7.2 0.8 compare_select_fusion.2
  8.0 0.7 compare_bitcast_fusion
  8.7 0.1 copy.13
  8.8 0.1 reshape.133
  8.9 0.1 copy.12
  9.0 4.6 %gather_fusion = bf16[1024,256]{1,0:T(8,128)(2,1)S(1)} fusion(bf16[1024,256]{1,0:T(8,128)(2,1)} %param.9, s32[1024]{0:T(1024)S(1)} %broadcast_clamp_fusion.2), kind=kCustom, calls=%fused_computation | custom fusion | bytes 1052672 | tf_op jit(solution)/shard_map/gather | solution.py:21
  13.6 1.0 bitcast_select_fusion
  14.6 19.5 %all-to-all-start = ((bf16[128,8,256]{2,1,0:T(8,128)(2,1)}), bf16[128,8,256]{2,1,0:T(8,128)(2,1)S(1)}, u32[]{:S(2)}, u32[]{:S(2)}) async-start(bf16[128,8,256]{2,1,0:T(8,128)(2,1)} %bitcast_select_fusion), calls=%async_computation | async-start | bytes 1048576 | tf_op jit(solution)/shard_map/all_to_all | solution.py:26
  34.1 0.0 reduce-scatter.2.cloned.1.call-start
  34.8 0.0 copy-done.4
  34.8 0.0 copy-done.5
  34.9 32.7 %all-to-all-done = bf16[128,8,256]{2,1,0:T(8,128)(2,1)S(1)} async-done(((bf16[128,8,256]{2,1,0:T(8,128)(2,1)}), bf16[128,8,256]{2,1,0:T(8,128)(2,1)S(1)}, u32[]{:S(2)}, u32[]{:S(2)}) %all-to-all-start) | async-done | bytes 524320 | tf_op jit(solution)/shard_map/all_to_all | solution.py:26
  67.6 0.0 copy-done.1
  67.6 0.1 pad_maximum_fusion
  67.7 76.8 %scatter_custom_fusion = f32[4096,256]{1,0:T(8,128)} fusion(s32[8192]{0:T(1024)S(1)} %bitcast.41, pred[8192]{0:T(1024)(128)(4,1)S(1)} %fusion.19, bf16[]{:T(256)} %constant.41.clone.1, f32[]{:T(128)} %constant.14.clone.1, bf16[2048,256]{1,0:T(8,128)(2,1)S(1)} %pad_maximum_fusion, s32[8192]{0:T(1024)S(1)} %broadcast_clamp_fusion.1), kind=kCustom, calls=%fused_computation.9 | custom fusion | flops 6291456 | bytes 5283846 | tf_op jit(solution)/shard_map/scatter-add | solution.py:34
  144.6 0.0 copy-start.7
  144.6 0.0 copy-start.3
  144.6 0.0 copy-start.6
  144.6 3.8 %convert_element_type.41 = bf16[4096,256]{1,0:T(8,128)(2,1)} convert(f32[4096,256]{1,0:T(8,128)} %scatter_custom_fusion) | non-fusion elementwise | flops 1048576 | bytes 6291456 | tf_op jit(solution)/shard_map/convert_element_type | solution.py:37
  148.3 0.0 reduce-scatter.2.cloned.1.call-update
  148.4 43.2 %scatter_custom_fusion.1 = f32[4096]{0:T(1024)S(1)} fusion(s32[8192]{0:T(1024)S(1)} %bitcast.42, f32[8192]{0:T(1024)S(1)} %fusion.25, f32[]{:T(128)} %constant.14.clone.1), kind=kCustom, calls=%fused_computation.50 | custom fusion | flops 8192 | bytes 16388 | tf_op jit(solution)/shard_map/scatter-add | solution.py:22
  191.6 0.0 copy-done.7
  191.6 13.1 %psum.7 = f32[4096]{0:T(1024)S(1)} all-reduce(f32[4096]{0:T(1024)S(1)} %scatter_custom_fusion.1), channel_id=1, replica_groups=mesh['dom'=128,'src'=4] {'src'}, use_global_device_ids=true, to_apply=%region_3.4 | all-reduce | flops 4096 | bytes 32768 | tf_op jit(solution)/shard_map/psum | solution.py:23
  204.8 0.0 copy-done.3
  204.8 0.3 fusion.29
  205.1 0.0 reduce-scatter.2.cloned.1.call-done
  205.1 0.0 copy-done
  205.1 0.0 copy-done.6
  205.1 2.6 multiply_convert_fusion
  207.7 0.3 fusion.12
  208.0 1.5 stack.2
  209.5 3.8 %all-to-all-start.1 = ((bf16[4,1024,256]{2,1,0:T(8,128)(2,1)}), bf16[4,1024,256]{2,1,0:T(8,128)(2,1)S(1)}, u32[]{:S(2)}, u32[]{:S(2)}) async-start(bf16[4,1024,256]{2,1,0:T(8,128)(2,1)} %stack.2), calls=%async_computation.2 | async-start | bytes 4194304 | tf_op jit(solution)/shard_map/all_to_all | solution.py:54
  213.3 22.6 %all-to-all-done.1 = bf16[4,1024,256]{2,1,0:T(8,128)(2,1)S(1)} async-done(((bf16[4,1024,256]{2,1,0:T(8,128)(2,1)}), bf16[4,1024,256]{2,1,0:T(8,128)(2,1)S(1)}, u32[]{:S(2)}, u32[]{:S(2)}) %all-to-all-start.1) | async-done | bytes 2097184 | tf_op jit(solution)/shard_map/all_to_all | solution.py:54
  235.9 76.1 %scatter_custom_fusion.2 = f32[2048,256]{1,0:T(8,128)} fusion(s32[8192]{0:T(1024)S(1)} %bitcast.40, pred[8192]{0:T(1024)(128)(4,1)S(1)} %fusion.19, bf16[]{:T(256)} %constant.41.clone.1, f32[]{:T(128)} %constant.14.clone.1, bf16[4096,256]{1,0:T(8,128)(2,1)S(1)} %bitcast.37, s32[8192]{0:T(1024)S(1)} %broadcast_clamp_fusion), kind=kCustom, calls=%fused_computation.7 | custom fusion | flops 6291456 | bytes 4235270 | tf_op jit(solution)/shard_map/scatter-add | solution.py:58
  312.0 2.1 fusion.16
  314.0 10.1 %all-to-all-start.2 = ((bf16[128,8,256]{2,1,0:T(8,128)(2,1)}), bf16[128,8,256]{2,1,0:T(8,128)(2,1)S(1)}, u32[]{:S(2)}, u32[]{:S(2)}) async-start(bf16[128,8,256]{2,1,0:T(8,128)(2,1)} %fusion.16), calls=%async_computation.3 | async-start | bytes 1048576 | tf_op jit(solution)/shard_map/all_to_all | solution.py:62
  324.1 0.1 copy.14
  324.2 0.1 reshape.181
  324.3 1.6 convolution_add_fusion
  325.9 31.8 %all-to-all-done.2 = bf16[128,8,256]{2,1,0:T(8,128)(2,1)S(1)} async-done(((bf16[128,8,256]{2,1,0:T(8,128)(2,1)}), bf16[128,8,256]{2,1,0:T(8,128)(2,1)S(1)}, u32[]{:S(2)}, u32[]{:S(2)}) %all-to-all-start.2) | async-done | bytes 524320 | tf_op jit(solution)/shard_map/all_to_all | solution.py:62
  357.7 6.5 %scatter_custom_fusion.3 = f32[1024,256]{1,0:T(8,128)S(1)} fusion(f32[1024,256]{1,0:T(8,128)S(1)} %convolution_add_fusion, s32[1024]{0:T(1024)S(1)} %reshape.181, bf16[128,8,256]{2,1,0:T(8,128)(2,1)S(1)} %all-to-all-done.2), kind=kCustom, calls=%fused_computation.25 | custom fusion | flops 524288 | bytes 1572864 | tf_op jit(solution)/shard_map/scatter-add | solution.py:71
  364.2 0.0 copy-start.2
  364.2 1.0 copy-done.2
  (9 shorter events, 0.1 us)
Async XLA Ops:
  7.2 197.9 %copy-start = (bf16[256,256]{1,0:T(8,128)(2,1)S(1)}, bf16[256,256]{1,0:T(8,128)(2,1)}, u32[]{:S(2)}) copy-start(bf16[256,256]{1,0:T(8,128)(2,1)} %param.12) | copy-start | bytes 393220
  7.2 60.5 %copy-start.1 = (bf16[1024,256]{1,0:T(8,128)(2,1)S(1)}, bf16[1024,256]{1,0:T(8,128)(2,1)}, u32[]{:S(2)}) copy-start(bf16[1024,256]{1,0:T(8,128)(2,1)} %param.9) | copy-start | bytes 1572868
  7.2 27.6 %copy-start.4 = (s32[1,1,8192]{2,1,0:T(1,128)S(1)}, s32[1,1,8192]{2,1,0:T(1,128)}, u32[]{:S(2)}) copy-start(s32[1,1,8192]{2,1,0:T(1,128)} %param.15) | copy-start | bytes 98308
  7.2 27.6 %copy-start.5 = (s32[1,1,8192]{2,1,0:T(1,128)S(1)}, s32[1,1,8192]{2,1,0:T(1,128)}, u32[]{:S(2)}) copy-start(s32[1,1,8192]{2,1,0:T(1,128)} %param.16) | copy-start | bytes 98308
  14.6 53.1 %all-to-all-start = ((bf16[128,8,256]{2,1,0:T(8,128)(2,1)}), bf16[128,8,256]{2,1,0:T(8,128)(2,1)S(1)}, u32[]{:S(2)}, u32[]{:S(2)}) async-start(bf16[128,8,256]{2,1,0:T(8,128)(2,1)} %bitcast_select_fusion), calls=%async_computation | async-start | bytes 1048576 | tf_op jit(solution)/shard_map/all_to_all | solution.py:26
  34.1 171.0 %reduce-scatter.2.cloned.1.call-start = ((), (), s32[]{:S(2)}) async-start(), calls=%async_computation.4 | async-start | bytes 2621440 | tf_op jit(solution)/shard_map/reduce_scatter | solution.py:36
  144.6 47.0 %copy-start.7 = (bf16[256]{0:T(256)(128)(2,1)S(1)}, bf16[256]{0:T(256)(128)(2,1)}, u32[]{:S(2)}) copy-start(bf16[256]{0:T(256)(128)(2,1)} %param.13) | copy-start | bytes 1540
  144.6 60.2 %copy-start.3 = (bf16[256,256]{1,0:T(8,128)(2,1)S(1)}, bf16[256,256]{1,0:T(8,128)(2,1)}, u32[]{:S(2)}) copy-start(bf16[256,256]{1,0:T(8,128)(2,1)} %param.11) | copy-start | bytes 393220
  144.6 60.5 %copy-start.6 = (bf16[1024,256]{1,0:T(8,128)(2,1)S(1)}, bf16[1024,256]{1,0:T(8,128)(2,1)}, u32[]{:S(2)}) copy-start(bf16[1024,256]{1,0:T(8,128)(2,1)} %param.10) | copy-start | bytes 1572868
  209.5 26.4 %all-to-all-start.1 = ((bf16[4,1024,256]{2,1,0:T(8,128)(2,1)}), bf16[4,1024,256]{2,1,0:T(8,128)(2,1)S(1)}, u32[]{:S(2)}, u32[]{:S(2)}) async-start(bf16[4,1024,256]{2,1,0:T(8,128)(2,1)} %stack.2), calls=%async_computation.2 | async-start | bytes 4194304 | tf_op jit(solution)/shard_map/all_to_all | solution.py:54
  314.0 43.6 %all-to-all-start.2 = ((bf16[128,8,256]{2,1,0:T(8,128)(2,1)}), bf16[128,8,256]{2,1,0:T(8,128)(2,1)S(1)}, u32[]{:S(2)}, u32[]{:S(2)}) async-start(bf16[128,8,256]{2,1,0:T(8,128)(2,1)} %fusion.16), calls=%async_computation.3 | async-start | bytes 1048576 | tf_op jit(solution)/shard_map/all_to_all | solution.py:62
  364.2 1.0 copy-start.2
Sparse Core Ops, SparseCore 0:
  148.5 28.3 reduce-scatter.1
